TPU v7x, 32 devices: a whole 2x2x4 slice. The times are simulated.
32 devices in a mesh: row: 8 (over y, x, core), col: 4 (over z).
Axes of the slice: x: 2, y: 2, z: 4, core: 2. Of those that a mesh axis runs over, the one named last changes fastest.
Arguments:
- panel: bfloat16 [24576, 256], P('row', 'col'), as said below
- trailing: bfloat16 [24576, 16384], P('row', 'col'), may hold values from -6 to 6
- tile_list: int32 [176], P('row'), may hold values from 0 to 23, as said below
Outputs:
- triangle: float32 [256, 256], replicated
- top_rows: float32 [16384, 256], P('col')
- updated: bfloat16 [22528, 16384], P('row', 'col')
Inputs may be any that keep to these rules, and one draw needn't show every extreme that they name: `tile_list`: each aligned block of 22 entries (the entries of one index of row) lists distinct tile numbers of that group's 24 tiles in increasing order and always includes tile 24 - 1. `panel`: the active rows of every row group, and all active rows together, have full column rank with a condition number under 100.
All inputs are finite; a program needn't handle non-finite values.
Results may differ from a plain program's by a relative error of at most 0.0065.
Values may be sent and summed in bfloat16 or wider, within the bound.
No kernel may reach another device: no remote copies, remote signals or barrier semaphores. Data moves between devices by JAX's collectives and lax.ppermute only.
A program may use at most 128 MiB of HBM per device.

v0:
```python
import jax
import jax.numpy as jnp
from jax import lax
from jax.sharding import PartitionSpec as P

TILE = 128


def pick_tiles(whole, tile_list):
    tiled = whole.reshape(-1, TILE, whole.shape[1])
    return jnp.take(tiled, tile_list, axis=0).reshape(-1, whole.shape[1])


def local(panel, trailing, tile_list):
    panel_full = lax.all_gather(panel, "col", axis=1, tiled=True)
    act_panel = pick_tiles(panel_full, tile_list)
    act_trail = pick_tiles(trailing, tile_list)
    local_gram = lax.dot_general(
        act_panel, act_panel, (((0,), (0,)), ((), ())), preferred_element_type=jnp.float32
    )
    gram_matrix = lax.psum(local_gram.astype(jnp.bfloat16), "row").astype(jnp.float32)
    lower_factor = jnp.linalg.cholesky(gram_matrix)
    triangle = lower_factor.T
    local_cross = lax.dot_general(
        act_trail, act_panel, (((0,), (0,)), ((), ())), preferred_element_type=jnp.float32
    )
    cross_sum = lax.psum(local_cross, "row")
    top_rows = jax.scipy.linalg.solve_triangular(lower_factor, cross_sum.T, lower=True).T
    coeff = jax.scipy.linalg.solve_triangular(
        lower_factor, top_rows.T, lower=True, trans=1
    ).T.astype(jnp.bfloat16)
    product = lax.dot_general(
        act_panel, coeff, (((1,), (1,)), ((), ())), preferred_element_type=jnp.float32
    )
    updated = (act_trail.astype(jnp.float32) - product).astype(jnp.bfloat16)
    return (triangle, top_rows, updated)


def solution(mesh):
    return jax.shard_map(
        local,
        mesh=mesh,
        in_specs=(P("row", "col"), P("row", "col"), P("row")),
        out_specs=(P(), P("col", None), P("row", "col")),
        check_vma=False,
    )
```

profile of v0, /device:TPU:0, one launch (start us, length us, event | category | flops | bytes accessed | tf_op | source)
XLA Modules:
  0.0 239.5 jit_solution(15465657170109536758)
XLA Ops:
  7.2 0.7 all-gather.2.cloned.1.call-update
  7.9 0.7 compare_and_fusion
  8.6 0.7 compare_select_fusion
  9.4 17.7 %gather_fusion.1 = bf16[22,128,4096]{2,1,0:T(8,128)(2,1)} fusion(bf16[24,128,4096]{2,1,0:T(8,128)(2,1)} %bitcast.57, s32[1024]{0:T(1024)S(1)} %pad_clamp_fusion), kind=kCustom, calls=%fused_computation.1 | custom fusion | bytes 46137432 | tf_op jit(solution)/shard_map/jit(_take)/gather | solution.py:11
  27.1 20.6 %bitcast_select_fusion = bf16[2816,4096]{1,0:T(8,128)(2,1)} fusion(bf16[22,128,4096]{2,1,0:T(8,128)(2,1)} %gather_fusion.1, pred[2816]{0:T(1024)(128)(4,1)S(1)} %broadcast_bitcast_fusion), kind=kLoop, calls=%fused_computation.5 | loop fusion | flops 11534336 | bytes 46140160 | tf_op jit(solution)/shard_map/jit(_take)/select_n | solution.py:11
  47.7 1.6 all-gather.2.cloned.1.call-done
  49.3 1.7 copy.11
  51.7 1.5 fusion.12
  53.2 12.2 %fusion.4 = f32[256,4096]{1,0:T(8,128)} fusion(bf16[22,128,4096]{2,1,0:T(8,128)(2,1)} %gather_fusion.1, pred[22]{0:T(512)(128)(4,1)S(1)} %compare_and_fusion, bf16[22,128,256]{2,1,0:T(8,128)(2,1)S(1)} %gather_fusion), kind=kOutput, calls=%fused_computation.10 | convolution fusion | flops 5917835264 | bytes 28704790 | tf_op jit(solution)/shard_map/dot_general | solution.py:24
  65.4 1.7 bitcast_select_fusion.1
  67.1 40.8 %all-reduce.4.cloned.1.call-done = bf16[256,256]{0,1:T(8,128)(2,1)} async-done(((bf16[256,256]{0,1:T(8,128)(2,1)}), bf16[256,256]{0,1:T(8,128)(2,1)}) %all-reduce.4.cloned.1.call-update) | async-done | bytes 131088 | tf_op jit(solution)/shard_map/psum | solution.py:21
  107.9 1.0 copy.14
  108.9 0.9 fusion.13
  109.9 11.7 %cholesky.50 = f32[128,128]{1,0:T(8,128)S(1)} custom-call(f32[128,128]{1,0:T(8,128)S(1)} %cholesky.118), custom_call_target="Cholesky" | custom-call | tf_op jit(solution)/shard_map/jit(cholesky)/cholesky | solution.py:22
  121.6 9.8 %custom-call.18 = f32[1,128,128]{1,2,0:T(8,128)S(1)} custom-call(f32[1,128,128]{2,1,0:T(8,128)S(1)} %get-tuple-element.32), custom_call_target="InvertDiagBlocksLowerTriangular" | custom-call | tf_op jit(solution)/shard_map/jit(cholesky)/cholesky | solution.py:22
  131.9 11.7 %cholesky.105 = f32[128,128]{1,0:T(8,128)S(1)} custom-call(f32[128,128]{1,0:T(8,128)S(1)} %convolution_subtract_fusion.2), custom_call_target="Cholesky" | custom-call | tf_op jit(solution)/shard_map/jit(cholesky)/cholesky | solution.py:22
  143.7 0.6 compare_reduce_fusion
  145.7 0.8 copy.16
  146.6 4.0 %while.1 = (s32[]{:T(128)}, f32[256,256]{1,0:T(8,128)S(1)}, s32[2,2]{1,0:T(2,128)S(1)}, f32[2,128,128]{2,1,0:T(8,128)S(1)}, s32[]{:T(128)}) while((s32[]{:T(128)}, f32[256,256]{1,0:T(8,128)S(1)}, s32[2,2]{1,0:T(2,128)S(1)}, f32[2,128,128]{2,1,0:T(8,128)S(1)}, s32[]{:T(128)}) %tuple.31), condition=%wide.while_cond, body=%wide.while_body.sunk | while | flops 2 | bytes 131189 | solution.py:28
  147.2 1.4 bitcast_dynamic-update-slice_fusion.2
  149.2 1.4 bitcast_dynamic-update-slice_fusion.2
  150.6 19.9 %custom-call.19 = f32[2,128,128]{1,2,0:T(8,128)S(1)} custom-call(f32[2,128,128]{2,1,0:T(8,128)S(1)} %get-tuple-element.10), custom_call_target="InvertDiagBlocksLowerTriangular" | custom-call | tf_op jit(solution)/shard_map/jit(_solve_triangular)/triangular_solve | solution.py:28
  170.5 21.7 %all-reduce.6.cloned.1.call-done = f32[256,4096]{1,0:T(8,128)} async-done(((f32[256,4096]{1,0:T(8,128)}), f32[256,4096]{1,0:T(8,128)}) %all-reduce.6.cloned.1.call-update) | async-done | bytes 4194320 | tf_op jit(solution)/shard_map/psum | solution.py:27
  192.2 3.6 %fusion.7 = f32[128,4096]{1,0:T(8,128)S(1)} fusion(f32[256,4096]{1,0:T(8,128)} %all-reduce.6.cloned.1.call-done, f32[2,128,128]{1,2,0:T(8,128)S(1)} %custom-call.19), kind=kOutput, calls=%fused_computation.15 | convolution fusion | flops 805306368 | bytes 4259840 | tf_op jit(solution)/shard_map/jit(_solve_triangular)/triangular_solve | solution.py:28
  195.9 1.9 convolution_subtract_fusion.1
  197.8 1.9 fusion.20
  199.8 1.9 fusion.27
  201.7 2.5 %maximum_bitcast_fusion = f32[4096,256]{0,1:T(8,128)} fusion(f32[128,4096]{1,0:T(8,128)S(1)} %fusion.20, f32[128,4096]{1,0:T(8,128)S(1)} %fusion.7), kind=kLoop, calls=%fused_computation.14 | loop fusion | flops 1048576 | bytes 8388608 | tf_op jit(solution)/shard_map/transpose | solution.py:28
  204.2 2.0 convolution_subtract_fusion
  206.2 1.9 convolution_convert_fusion
  208.1 5.9 %copy.17 = f32[4096,256]{1,0:T(8,128)} copy(f32[4096,256]{0,1:T(8,128)} %maximum_bitcast_fusion) | data formatting | bytes 8388608
  213.9 19.1 %subtract_convert_fusion = bf16[2816,4096]{1,0:T(8,128)(2,1)} fusion(bf16[2816,4096]{1,0:T(8,128)(2,1)} %bitcast_select_fusion, bf16[2816,256]{1,0:T(8,128)(2,1)S(1)} %bitcast_select_fusion.1, bf16[128,4096]{1,0:T(8,128)(2,1)S(1)} %get-tuple-element.35, bf16[128,4096]{1,0:T(8,128)(2,1)S(1)} %convolution_convert_fusion), kind=kOutput, calls=%fused_computation.4 | convolution fusion | flops 5944377344 | bytes 49676288 | tf_op jit(solution)/shard_map/dot_general | solution.py:32
  (28 shorter events, 2.7 us)
Async XLA Ops:
  7.2 42.2 %all-gather.2.cloned.1.call-start = ((), (), s32[]{:S(2)}) async-start(), calls=%async_computation | async-start | bytes 1966080 | tf_op jit(solution)/shard_map/all_gather | solution.py:15
  7.9 100.0 %all-reduce.4.cloned.1.call-start = ((), (), s32[]{:S(2)}) async-start(), calls=%async_computation.1 | async-start | bytes 262144 | tf_op jit(solution)/shard_map/psum | solution.py:21
  53.2 139.0 %all-reduce.6.cloned.1.call-start = ((), (), s32[]{:S(2)}) async-start(), calls=%async_computation.2 | async-start | bytes 8388608 | tf_op jit(solution)/shard_map/psum | solution.py:27
  170.5 29.2 %copy-start.1 = (f32[2,128,128]{1,2,0:T(8,128)}, f32[2,128,128]{1,2,0:T(8,128)S(1)}, u32[]{:S(2)}) copy-start(f32[2,128,128]{1,2,0:T(8,128)S(1)} %custom-call.19) | copy-start | bytes 393220
  192.2 3.7 %copy-start = (f32[256,4096]{1,0:T(8,128)S(1)}, f32[256,4096]{1,0:T(8,128)}, u32[]{:S(2)}) copy-start(f32[256,4096]{1,0:T(8,128)} %all-reduce.6.cloned.1.call-done) | copy-start | bytes 12582916
  204.2 2.0 copy-start.2
Sparse Core Ops, SparseCore 0:
  9.5 39.7 all-gather.1
  53.3 54.5 all-reduce.3
  111.7 80.4 all-reduce.5
where the time goes:
time: 240 us
  other arithmetic  80.9 us (34%)
  waiting for transfers between devices  64.8 us (27%)
  matrix products  46.5 us (19%)
  local copies, waits for them, and re-layouts  31.9 us (13%)
  between operations  15.2 us (6%)
    psum x1, waiting for transfers between devices, local(): lax.psum(local_gram.astype(jnp.bfloat16), 'row').astype(jnp.float32)  40.8 us
    another operation x6, other arithmetic, local(): lower_factor = jnp.linalg.cholesky(gram_matrix)  34 us
    select_n x3, other arithmetic, pick_tiles(): return jnp.take(tiled, tile_list, axis=0).reshape(-1, whole.shape[1])  22.9 us
    psum x1, waiting for transfers between devices, local(): cross_sum = lax.psum(local_cross, 'row')  21.7 us
    another operation x3, other arithmetic, local(): jax.scipy.linalg.solve_triangular(lower_factor, cross_sum.T, lower=True)  19.9 us
    dot_general x1, matrix products, local(): lax.dot_general(act_panel, coeff, (((1,), (1,)), ((), ())), preferred_ele...  19.1 us
    gather x2, local copies, waits for them, and re-layouts, pick_tiles(): return jnp.take(tiled, tile_list, axis=0).reshape(-1, whole.shape[1])  18.4 us
    dot_general x1, matrix products, local(): lax.dot_general(act_trail, act_panel, (((0,), (0,)), ((), ())), preferred...  12.2 us
  transfers between devices with their start and end apart: 3, of which 3 were waited for; matrix products, arithmetic and copies ran while one was open for 48% of the time, Pallas kernels for 0%

commit v1 on v0

--- a/solution.py
+++ b/solution.py
@@ -18,7 +18,9 @@
     local_gram = lax.dot_general(
         act_panel, act_panel, (((0,), (0,)), ((), ())), preferred_element_type=jnp.float32
     )
-    gram_matrix = lax.psum(local_gram.astype(jnp.bfloat16), "row").astype(jnp.float32)
+    gram_matrix = jnp.sum(lax.all_gather(local_gram.astype(jnp.bfloat16), "row"), axis=0).astype(
+        jnp.float32
+    )
     lower_factor = jnp.linalg.cholesky(gram_matrix)
     triangle = lower_factor.T
     local_cross = lax.dot_general(

time: 240 us -> 211 us (0.88)
  waiting for transfers between devices: 64.8 us -> 35.7 us
    psum x1 -> x0, waiting for transfers between devices: 40.8 us -> none  [local(): lax.psum(local_gram.astype(jnp.bfloat16), 'row').astype(jnp.float32)]
    all_gather x0 -> x1, waiting for transfers between devices: none -> 10.8 us  [local(): lax.all_gather(local_gram.astype(jnp.bfloat16), 'row')]
  transfers between devices with their start and end apart: 3 -> 3, of which waited for: 3 -> 3; matrix products, arithmetic and copies ran while one was open for 48% -> 54% of each run, Pallas kernels for 0% -> 0%
where the time goes in v1:
time: 211 us; the launch traced here: 210 us
  other arithmetic  81.4 us (39%)
  matrix products  46.5 us (22%)
  waiting for transfers between devices  35.7 us (17%)
  local copies, waits for them, and re-layouts  31.1 us (15%)
  between operations  15.2 us (7%)
    another operation x6, other arithmetic, local(): lower_factor = jnp.linalg.cholesky(gram_matrix)  34 us
    select_n x3, other arithmetic, pick_tiles(): return jnp.take(tiled, tile_list, axis=0).reshape(-1, whole.shape[1])  22.9 us
    psum x1, waiting for transfers between devices, local(): cross_sum = lax.psum(local_cross, 'row')  22.6 us
    another operation x3, other arithmetic, local(): jax.scipy.linalg.solve_triangular(lower_factor, cross_sum.T, lower=True)  19.9 us
    dot_general x1, matrix products, local(): lax.dot_general(act_panel, coeff, (((1,), (1,)), ((), ())), preferred_ele...  19.1 us
    gather x2, local copies, waits for them, and re-layouts, pick_tiles(): return jnp.take(tiled, tile_list, axis=0).reshape(-1, whole.shape[1])  18.4 us
    dot_general x1, matrix products, local(): lax.dot_general(act_trail, act_panel, (((0,), (0,)), ((), ())), preferred...  12.1 us
    all_gather x1, waiting for transfers between devices, local(): lax.all_gather(local_gram.astype(jnp.bfloat16), 'row')  10.8 us
  transfers between devices with their start and end apart: 3, of which 3 were waited for; matrix products, arithmetic and copies ran while one was open for 54% of the time, Pallas kernels for 0%

profile of v1, /device:TPU:0, one launch (start us, length us, event | category | flops | bytes accessed | tf_op | source)
XLA Modules:
  0.0 210.2 jit_solution(8633984732473702305)
XLA Ops:
  7.2 0.7 all-gather.4.cloned.1.call-update
  7.9 0.7 compare_and_fusion
  8.6 0.7 compare_select_fusion
  9.4 17.7 %gather_fusion.1 = bf16[22,128,4096]{2,1,0:T(8,128)(2,1)} fusion(bf16[24,128,4096]{2,1,0:T(8,128)(2,1)} %bitcast.58, s32[1024]{0:T(1024)S(1)} %pad_clamp_fusion), kind=kCustom, calls=%fused_computation.1 | custom fusion | bytes 46137432 | tf_op jit(solution)/shard_map/jit(_take)/gather | solution.py:11
  27.1 20.6 %bitcast_select_fusion = bf16[2816,4096]{1,0:T(8,128)(2,1)} fusion(bf16[22,128,4096]{2,1,0:T(8,128)(2,1)} %gather_fusion.1, pred[2816]{0:T(1024)(128)(4,1)S(1)} %broadcast_bitcast_fusion), kind=kLoop, calls=%fused_computation.5 | loop fusion | flops 11534336 | bytes 46140160 | tf_op jit(solution)/shard_map/jit(_take)/select_n | solution.py:11
  47.7 1.6 all-gather.4.cloned.1.call-done
  49.3 1.7 copy.16
  51.0 0.6 gather_fusion
  51.7 1.5 fusion.12
  53.3 12.1 %fusion.4 = f32[256,4096]{1,0:T(8,128)} fusion(bf16[22,128,4096]{2,1,0:T(8,128)(2,1)} %gather_fusion.1, pred[22]{0:T(512)(128)(4,1)S(1)} %compare_and_fusion, bf16[22,128,256]{2,1,0:T(8,128)(2,1)S(1)} %gather_fusion), kind=kOutput, calls=%fused_computation.10 | convolution fusion | flops 5917835264 | bytes 28704790 | tf_op jit(solution)/shard_map/dot_general | solution.py:26
  65.5 1.7 bitcast_select_fusion.1
  67.1 10.8 %all-gather.6.cloned.1.call-done = bf16[2048,256]{1,0:T(8,128)(2,1)} async-done(((bf16[256,256]{1,0:T(8,128)(2,1)}), bf16[2048,256]{1,0:T(8,128)(2,1)}) %all-gather.6.cloned.1.call-update) | async-done | bytes 1048592 | tf_op jit(solution)/shard_map/all_gather | solution.py:21
  77.9 1.4 reduce_sum.12
  79.5 11.7 %cholesky.50 = f32[128,128]{1,0:T(8,128)S(1)} custom-call(f32[128,128]{1,0:T(8,128)S(1)} %cholesky.118), custom_call_target="Cholesky" | custom-call | tf_op jit(solution)/shard_map/jit(cholesky)/cholesky | solution.py:24
  91.3 9.8 %custom-call.18 = f32[1,128,128]{1,2,0:T(8,128)S(1)} custom-call(f32[1,128,128]{2,1,0:T(8,128)S(1)} %get-tuple-element.35), custom_call_target="InvertDiagBlocksLowerTriangular" | custom-call | tf_op jit(solution)/shard_map/jit(cholesky)/cholesky | solution.py:24
  101.6 11.7 %cholesky.105 = f32[128,128]{1,0:T(8,128)S(1)} custom-call(f32[128,128]{1,0:T(8,128)S(1)} %convolution_subtract_fusion.2), custom_call_target="Cholesky" | custom-call | tf_op jit(solution)/shard_map/jit(cholesky)/cholesky | solution.py:24
  113.3 0.6 compare_reduce_fusion
  115.3 0.8 copy.21
  116.2 4.0 %while.1 = (s32[]{:T(128)}, f32[256,256]{1,0:T(8,128)S(1)}, s32[2,2]{1,0:T(2,128)S(1)}, f32[2,128,128]{2,1,0:T(8,128)S(1)}, s32[]{:T(128)}) while((s32[]{:T(128)}, f32[256,256]{1,0:T(8,128)S(1)}, s32[2,2]{1,0:T(2,128)S(1)}, f32[2,128,128]{2,1,0:T(8,128)S(1)}, s32[]{:T(128)}) %tuple.32), condition=%wide.while_cond, body=%wide.while_body.sunk | while | flops 2 | bytes 131189 | solution.py:30
  116.8 1.4 bitcast_dynamic-update-slice_fusion.2
  118.9 1.4 bitcast_dynamic-update-slice_fusion.2
  120.3 19.9 %custom-call.19 = f32[2,128,128]{1,2,0:T(8,128)S(1)} custom-call(f32[2,128,128]{2,1,0:T(8,128)S(1)} %get-tuple-element.10), custom_call_target="InvertDiagBlocksLowerTriangular" | custom-call | tf_op jit(solution)/shard_map/jit(_solve_triangular)/triangular_solve | solution.py:30
  140.2 22.6 %all-reduce.3.cloned.1.call-done = f32[256,4096]{1,0:T(8,128)} async-done(((f32[256,4096]{1,0:T(8,128)}), f32[256,4096]{1,0:T(8,128)}) %all-reduce.3.cloned.1.call-update) | async-done | bytes 4194320 | tf_op jit(solution)/shard_map/psum | solution.py:29
  162.8 3.6 %fusion.7 = f32[128,4096]{1,0:T(8,128)S(1)} fusion(f32[256,4096]{1,0:T(8,128)} %all-reduce.3.cloned.1.call-done, f32[2,128,128]{1,2,0:T(8,128)S(1)} %custom-call.19), kind=kOutput, calls=%fused_computation.15 | convolution fusion | flops 805306368 | bytes 4259840 | tf_op jit(solution)/shard_map/jit(_solve_triangular)/triangular_solve | solution.py:30
  166.5 1.9 convolution_subtract_fusion.1
  168.4 1.9 fusion.20
  170.4 1.9 fusion.27
  172.3 2.5 %maximum_bitcast_fusion = f32[4096,256]{0,1:T(8,128)} fusion(f32[128,4096]{1,0:T(8,128)S(1)} %fusion.20, f32[128,4096]{1,0:T(8,128)S(1)} %fusion.7), kind=kLoop, calls=%fused_computation.14 | loop fusion | flops 1048576 | bytes 8388608 | tf_op jit(solution)/shard_map/transpose | solution.py:30
  174.8 2.0 convolution_subtract_fusion
  176.8 1.9 convolution_convert_fusion
  178.7 5.9 %copy.22 = f32[4096,256]{1,0:T(8,128)} copy(f32[4096,256]{0,1:T(8,128)} %maximum_bitcast_fusion) | data formatting | bytes 8388608
  184.6 19.1 %subtract_convert_fusion = bf16[2816,4096]{1,0:T(8,128)(2,1)} fusion(bf16[2816,4096]{1,0:T(8,128)(2,1)} %bitcast_select_fusion, bf16[2816,256]{1,0:T(8,128)(2,1)S(1)} %bitcast_select_fusion.1, bf16[128,4096]{1,0:T(8,128)(2,1)S(1)} %get-tuple-element.38, bf16[128,4096]{1,0:T(8,128)(2,1)S(1)} %convolution_convert_fusion), kind=kOutput, calls=%fused_computation.4 | convolution fusion | flops 5944377344 | bytes 49676288 | tf_op jit(solution)/shard_map/dot_general | solution.py:34
  (30 shorter events, 2.3 us)
Async XLA Ops:
  7.2 42.2 %all-gather.4.cloned.1.call-start = ((), (), s32[]{:S(2)}) async-start(), calls=%async_computation | async-start | bytes 1966080 | tf_op jit(solution)/shard_map/all_gather | solution.py:15
  7.9 70.0 %all-gather.6.cloned.1.call-start = ((), (), s32[]{:S(2)}) async-start(), calls=%async_computation.2 | async-start | bytes 1179648 | tf_op jit(solution)/shard_map/all_gather | solution.py:21
  53.2 109.6 %all-reduce.3.cloned.1.call-start = ((), (), s32[]{:S(2)}) async-start(), calls=%async_computation.1 | async-start | bytes 8388608 | tf_op jit(solution)/shard_map/psum | solution.py:29
  140.2 30.2 %copy-start.1 = (f32[2,128,128]{1,2,0:T(8,128)}, f32[2,128,128]{1,2,0:T(8,128)S(1)}, u32[]{:S(2)}) copy-start(f32[2,128,128]{1,2,0:T(8,128)S(1)} %custom-call.19) | copy-start | bytes 393220
  162.8 3.7 %copy-start = (f32[256,4096]{1,0:T(8,128)S(1)}, f32[256,4096]{1,0:T(8,128)}, u32[]{:S(2)}) copy-start(f32[256,4096]{1,0:T(8,128)} %all-reduce.3.cloned.1.call-done) | copy-start | bytes 12582916
  174.8 2.0 copy-start.2
Sparse Core Ops, SparseCore 0:
  9.5 39.7 all-gather.3
  53.4 24.4 all-gather.5
  81.7 81.0 all-reduce.2
